TPU v7x, 256 devices: a whole 4x4x8 slice. The times are simulated.
256 devices in a mesh: azim: 64 (over x, y_hi, z), axial: 4 (over y_lo, core).
Axes of the slice: x: 4, y: 4 (y_hi: 2, y_lo: 2; y = y_hi * 2 + y_lo), z: 8, core: 2. Of those that a mesh axis runs over, the one named last changes fastest.
Arguments:
- rhs: float32 [64, 48, 4, 128], P('azim', None, 'axial'), may hold values from -6 to 6
- coupling: float32 [64, 48, 4, 128], P('azim', None, 'axial'), may hold values from 0.2 to 0.5
- fwd_coupling: bfloat16 [64, 48, 48, 4, 128], P('azim', None, None, 'axial'), may hold values from -1 to 1
- bwd_coupling: bfloat16 [64, 48, 48, 4, 128], P('azim', None, None, 'axial'), may hold values from -1 to 1
- block_inverse: bfloat16 [64, 48, 48, 4, 128], P('azim', None, None, 'axial'), may hold values from -1 to 1
Outputs:
- correction: float32 [64, 48, 4, 128], P('azim', None, 'axial')
- remaining: float32 [64, 48, 4, 128], P('azim', None, 'axial')
All inputs are finite; a program needn't handle non-finite values.
Results may differ from a plain program's by a relative error of at most 0.0003.
Values sent between devices are 32-bit elements; how exact they have to be, the bound alone decides.
A program may use at most 128 MiB of HBM per device.

v0:
```python
import jax
import jax.numpy as jnp
from jax import lax
from jax.sharding import PartitionSpec as P

highest = lax.Precision.HIGHEST


def from_behind(value, axis, steps):
    count = lax.axis_size(axis)
    initial, last = (max(0, -steps), min(count, count - steps))
    return lax.ppermute(value, axis, [(source, source + steps) for source in range(initial, last)])


def from_root(shard, axis, root):
    mine = lax.axis_index(axis) == root
    return lax.psum(jnp.where(mine, shard, jnp.zeros_like(shard)), axis)


def extended(block, sides, width):
    for axis, dim in sides:
        count = lax.axis_size(axis)
        forward = [(i, i + 1) for i in range(count - 1)]
        backward = [(target, source) for source, target in forward]
        low = lax.ppermute(
            lax.slice_in_dim(block, block.shape[dim] - width, None, axis=dim), axis, forward
        )
        high = lax.ppermute(lax.slice_in_dim(block, 0, width, axis=dim), axis, backward)
        block = jnp.concatenate([low, block, high], axis=dim)
    return block


def cell_stride(one_block, carried, const_term):
    return const_term - jnp.einsum(
        "abl,al->bl", one_block.astype(jnp.float32), carried, precision=highest
    )


def compose_cells(blocks, sequence):
    running = None
    for position in sequence:
        one_block = blocks[position].astype(jnp.float32)
        running = -jnp.swapaxes(one_block, 0, 1)
    return running


def doubling_maps(local_map, reverse):
    size = lax.axis_size("azim")
    index = lax.axis_index("azim")
    levels = []
    current = local_map
    distance = 1
    while distance < size:
        if reverse:
            moved = from_behind(current, "azim", -distance)
            exists = index + distance < size
        else:
            moved = from_behind(current, "azim", distance)
            exists = index >= distance
        levels.append((current, distance))
        current = jnp.where(
            exists, jnp.einsum("bcl,cal->bal", current, moved, precision=highest), current
        )
        distance = distance * 2
    return (levels, current)


def doubling_entries(map_levels, local_offset, reverse):
    levels, final_map = map_levels
    size = lax.axis_size("azim")
    index = lax.axis_index("azim")
    running = local_offset
    for current, distance in levels:
        if reverse:
            moved = from_behind(running, "azim", -distance)
        else:
            moved = from_behind(running, "azim", distance)
        running = jnp.einsum("bcl,cl->bl", current, moved, precision=highest) + running
    if reverse:
        wrapped = from_root(running, "azim", 0)
    else:
        wrapped = from_root(running, "azim", size - 1)
    leaving = jnp.einsum("bcl,cl->bl", final_map, wrapped, precision=highest) + running
    if reverse:
        shifted = from_behind(leaving, "azim", -1)
        first_device = index == size - 1
    else:
        shifted = from_behind(leaving, "azim", 1)
        first_device = index == 0
    return jnp.where(first_device, wrapped, shifted)


def sweep(blocks, consts, map_levels, reverse):
    cell_count = blocks.shape[0]
    sequence = list(range(cell_count))
    if reverse:
        sequence = sequence[::-1]
    carried = jnp.zeros(consts.shape[1:], jnp.float32)
    for position in sequence:
        carried = cell_stride(blocks[position], carried, consts[position])
    local_offset = carried
    incoming_maps = doubling_entries(map_levels, local_offset, reverse)
    outputs = [None] * cell_count
    carried = incoming_maps
    for position in sequence:
        carried = cell_stride(blocks[position], carried, consts[position])
        outputs[position] = carried
    return jnp.stack(outputs)


def on_device(rhs, coupling, fwd_coupling, bwd_coupling, block_inverse):
    cell_count, block_width, _, position_total, radial_count = fwd_coupling.shape
    line_count = position_total * radial_count
    forward_blocks = fwd_coupling.reshape(cell_count, block_width, block_width, line_count)
    backward_blocks = bwd_coupling.reshape(cell_count, block_width, block_width, line_count)
    inverse_blocks = block_inverse.reshape(cell_count, block_width, block_width, line_count)
    source = rhs.reshape(cell_count, block_width, line_count)
    coupling_field = coupling.reshape(cell_count, block_width, line_count)
    forward_map = compose_cells(forward_blocks, list(range(cell_count)))
    backward_map = compose_cells(backward_blocks, list(range(cell_count))[::-1])
    forward_levels = None
    backward_levels = None
    forward_levels = doubling_maps(forward_map, False)
    backward_levels = doubling_maps(backward_map, True)

    def precondition(vector):
        consts = jnp.stack(
            [
                jnp.einsum(
                    "abl,al->bl",
                    inverse_blocks[0].astype(jnp.float32),
                    vector[0],
                    precision=highest,
                )
            ]
        )
        forward = sweep(forward_blocks, consts, forward_levels, False)
        return sweep(backward_blocks, forward, backward_levels, True)

    def stations_sum(field):
        grid = field.reshape(cell_count, block_width, position_total, radial_count)
        padded = extended(grid, (("axial", 2),), 1)
        return (padded[:, :, :-2] + padded[:, :, 2:]).reshape(cell_count, block_width, line_count)

    applied_once = precondition(source)
    middle = source - applied_once + coupling_field * stations_sum(applied_once)
    second = precondition(middle)
    correction = applied_once + second
    remaining = middle - second + coupling_field * stations_sum(second)
    return (correction.reshape(rhs.shape), remaining.reshape(rhs.shape))


def solution(mesh):
    return jax.shard_map(
        on_device,
        mesh=mesh,
        in_specs=(
            P("azim", None, "axial", None),
            P("azim", None, "axial", None),
            P("azim", None, None, "axial", None),
            P("azim", None, None, "axial", None),
            P("azim", None, None, "axial", None),
        ),
        out_specs=(P("azim", None, "axial", None), P("azim", None, "axial", None)),
        check_vma=False,
    )
```

profile of v0, /device:TPU:1, one launch (start us, length us, event | category | flops | bytes accessed | tf_op | source)
XLA Modules:
  0.0 2142.2 jit_solution(16091125914390163233)
XLA Ops:
  7.7 5.4 collective-permute-start.2
  19.5 17.9 collective-permute-done
  38.6 5.6 collective-permute-start.1
  48.5 7.0 multiply_reduce_fusion.26
  57.5 8.3 collective-permute-start.4
  65.9 5.0 collective-permute-start.3
  71.0 42.8 %collective-permute-done.3 = f32[48,128]{1,0:T(8,128)S(1)} collective-permute-done((f32[48,128]{1,0:T(8,128)S(1)}, f32[48,128]{1,0:T(8,128)S(1)}, u32[]{:S(2)}, u32[]{:S(2)}) %collective-permute-start.3) | collective-permute-done | bytes 24608 | tf_op jit(solution)/shard_map/ppermute | solution.py:12
  117.1 6.5 multiply_reduce_fusion.25
  126.8 9.3 collective-permute-start.6
  136.2 6.0 collective-permute-start.5
  143.2 17.2 collective-permute-done.6
  160.4 3.3 copy.28
  163.7 9.3 multiply_reduce_fusion.24
  176.3 38.1 %collective-permute-start.8 = (f32[48,48,128]{2,1,0:T(8,128)}, f32[48,48,128]{2,1,0:T(8,128)}, u32[]{:S(2)}, u32[]{:S(2)}) collective-permute-start(f32[48,48,128]{2,1,0:T(8,128)} %copy.30), channel_id=1, source_target_pairs={{0,32},{4,36},{8,40},{12,44},{16,48},{20,52},{24,56},{28,60},{32,6... | collective-permute-start | bytes 3538952 | tf_op jit(solution)/shard_map/ppermute | solution.py:12
  218.1 17.8 collective-permute-done.8
  239.2 9.4 multiply_reduce_fusion.23
  251.8 9.1 collective-permute-start.10
  261.0 3.8 collective-permute-start.9
  264.9 16.8 collective-permute-done.9
  281.8 3.3 copy.34
  285.1 9.3 multiply_reduce_fusion.22
  297.6 6.4 collective-permute-start.11
  306.6 3.3 fusion.9
  309.8 3.3 copy.40
  317.1 319.2 %psum.28 = f32[48,128]{1,0:T(8,128)S(1)} all-reduce(f32[48,128]{1,0:T(8,128)S(1)} %broadcast_select_fusion.2), channel_id=1, replica_groups=mesh['azim'=64,'axial'=4] {'azim'}, use_global_device_ids=true, to_apply=%region_0.1 | all-reduce | flops 6144 | bytes 49152 | tf_op jit(solution)/shard_map/psum | solution.py:17
  636.5 3.3 copy.37
  639.8 9.3 multiply_reduce_fusion.21
  656.6 3.6 collective-permute-done.13
  663.8 3.3 copy.41
  668.1 8.6 multiply_reduce_fusion.19
  676.7 3.3 copy.42
  682.8 7.7 collective-permute-done.16
  690.6 19.6 collective-permute-done.17
  713.5 9.3 multiply_reduce_fusion.18
  728.7 5.9 collective-permute-done.18
  734.7 12.6 collective-permute-done.19
  747.3 3.3 copy.46
  750.6 9.5 multiply_reduce_fusion.17
  766.2 12.0 collective-permute-done.20
  778.4 3.7 collective-permute-done.21
  782.1 3.3 copy.49
  785.4 9.4 multiply_reduce_fusion.16
  800.7 5.2 collective-permute-done.22
  805.9 9.6 collective-permute-done.23
  818.8 9.5 multiply_reduce_fusion.15
  832.8 343.0 %psum.29 = f32[48,128]{1,0:T(8,128)S(1)} all-reduce(f32[48,128]{1,0:T(8,128)S(1)} %broadcast_select_fusion), channel_id=1, replica_groups=mesh['azim'=64,'axial'=4] {'azim'}, use_global_device_ids=true, to_apply=%region_1.2 | all-reduce | flops 6144 | bytes 49152 | tf_op jit(solution)/shard_map/psum | solution.py:17
  1176.0 3.3 copy.55
  1179.3 9.3 multiply_reduce_fusion.14
  1189.9 3.6 collective-permute-done.25
  1195.8 108.7 %collective-permute-start.27 = (f32[1,48,1,128]{3,1,2,0:T(8,128)S(1)}, f32[1,48,1,128]{3,1,2,0:T(8,128)S(1)}, u32[]{:S(2)}, u32[]{:S(2)}) collective-permute-start(f32[1,48,1,128]{3,1,2,0:T(8,128)S(1)} %subtract_bitcast_fusion.5), channel_id=1, source_target_pairs={{1,0},{2,1},{3,2},{5,4},{6,5},{7,6},{9,8},{10,9},{11,10},{13,12},{... | collective-permute-start | bytes 73736 | tf_op jit(solution)/shard_map/ppermute | solution.py:28
  1313.5 3.4 collective-permute-start.29
  1319.0 5.7 collective-permute-start.30
  1328.2 4.9 collective-permute-start.31
  1335.2 3.6 collective-permute-start.32
  1342.4 4.0 collective-permute-start.33
  1348.5 300.0 %psum.30 = f32[48,128]{1,0:T(8,128)S(1)} all-reduce(f32[48,128]{1,0:T(8,128)S(1)} %broadcast_select_fusion.1), channel_id=1, replica_groups=mesh['azim'=64,'axial'=4] {'azim'}, use_global_device_ids=true, to_apply=%region_2.3 | all-reduce | flops 6144 | bytes 49152 | tf_op jit(solution)/shard_map/psum | solution.py:17
  1657.1 3.5 collective-permute-done.35
  1664.4 4.0 collective-permute-done.36
  1671.2 7.5 collective-permute-done.37
  1682.6 5.1 collective-permute-done.38
  1690.4 3.4 collective-permute-done.39
  1697.7 4.8 collective-permute-done.40
  1703.7 296.5 %psum.31 = f32[48,128]{1,0:T(8,128)S(1)} all-reduce(f32[48,128]{1,0:T(8,128)S(1)} %broadcast_select_fusion.3), channel_id=1, replica_groups=mesh['azim'=64,'axial'=4] {'azim'}, use_global_device_ids=true, to_apply=%region_3.4 | all-reduce | flops 6144 | bytes 49152 | tf_op jit(solution)/shard_map/psum | solution.py:17
  2008.5 128.7 %collective-permute-start.43 = (f32[1,48,1,128]{3,1,2,0:T(8,128)S(1)}, f32[1,48,1,128]{3,1,2,0:T(8,128)S(1)}, u32[]{:S(2)}, u32[]{:S(2)}) collective-permute-start(f32[1,48,1,128]{3,1,2,0:T(8,128)S(1)} %subtract_bitcast_fusion.4), channel_id=1, source_target_pairs={{1,0},{2,1},{3,2},{5,4},{6,5},{7,6},{9,8},{10,9},{11,10},{13,12},{... | collective-permute-start | bytes 73736 | tf_op jit(solution)/shard_map/ppermute | solution.py:28
  (220 shorter events, 161.6 us)
Async XLA Ops:
  2.5 35.1 %copy-start.5 = (bf16[1,48,48,1,128]{2,1,4,3,0:T(8,128)(2,1)}, bf16[1,48,48,1,128]{2,1,4,3,0:T(8,128)(2,1)S(1)}, u32[]{:S(2)}) copy-start(bf16[1,48,48,1,128]{2,1,4,3,0:T(8,128)(2,1)S(1)} %copy.21) | copy-start | bytes 1769476
  4.5 11.2 copy-start.8
  7.7 37.5 %collective-permute-start.2 = (f32[48,48,128]{2,1,0:T(8,128)}, f32[48,48,128]{2,1,0:T(8,128)}, u32[]{:S(2)}, u32[]{:S(2)}) collective-permute-start(f32[48,48,128]{2,1,0:T(8,128)} %copy.22), channel_id=1, source_target_pairs={{0,4},{4,8},{8,12},{12,16},{16,20},{20,24},{24,28},{28,32},{32,36}... | collective-permute-start | bytes 3538952 | tf_op jit(solution)/shard_map/ppermute | solution.py:12
  15.0 30.3 %copy-start.6 = (bf16[128,48,48]{2,1,0:T(8,128)(2,1)}, bf16[128,48,48]{2,1,0:T(8,128)(2,1)S(1)}, u32[]{:S(2)}) copy-start(bf16[128,48,48]{2,1,0:T(8,128)(2,1)S(1)} %copy.68) | copy-start | bytes 1769476
  17.0 20.5 collective-permute-start
  38.6 6.5 collective-permute-start.1
  57.5 56.3 %collective-permute-start.4 = (f32[48,48,128]{2,1,0:T(8,128)}, f32[48,48,128]{2,1,0:T(8,128)}, u32[]{:S(2)}, u32[]{:S(2)}) collective-permute-start(f32[48,48,128]{2,1,0:T(8,128)} %copy.24), channel_id=1, source_target_pairs={{0,8},{4,12},{8,16},{12,20},{16,24},{20,28},{24,32},{28,36},{32,40... | collective-permute-start | bytes 3538952 | tf_op jit(solution)/shard_map/ppermute | solution.py:12
  65.9 47.8 %collective-permute-start.3 = (f32[48,128]{1,0:T(8,128)S(1)}, f32[48,128]{1,0:T(8,128)S(1)}, u32[]{:S(2)}, u32[]{:S(2)}) collective-permute-start(f32[48,128]{1,0:T(8,128)S(1)} %bitcast_add_fusion.29), channel_id=1, source_target_pairs={{0,16},{4,20},{8,24},{12,28},{16,32},{20,36},{24,40},{28,44},{32,4... | collective-permute-start | bytes 73736 | tf_op jit(solution)/shard_map/ppermute | solution.py:12
  126.8 33.5 %collective-permute-start.6 = (f32[48,48,128]{2,1,0:T(8,128)}, f32[48,48,128]{2,1,0:T(8,128)}, u32[]{:S(2)}, u32[]{:S(2)}) collective-permute-start(f32[48,48,128]{2,1,0:T(8,128)} %copy.27), channel_id=1, source_target_pairs={{0,16},{4,20},{8,24},{12,28},{16,32},{20,36},{24,40},{28,44},{32,4... | collective-permute-start | bytes 3538952 | tf_op jit(solution)/shard_map/ppermute | solution.py:12
  136.2 6.9 collective-permute-start.5
  176.3 59.7 %collective-permute-start.8 = (f32[48,48,128]{2,1,0:T(8,128)}, f32[48,48,128]{2,1,0:T(8,128)}, u32[]{:S(2)}, u32[]{:S(2)}) collective-permute-start(f32[48,48,128]{2,1,0:T(8,128)} %copy.30), channel_id=1, source_target_pairs={{0,32},{4,36},{8,40},{12,44},{16,48},{20,52},{24,56},{28,60},{32,6... | collective-permute-start | bytes 3538952 | tf_op jit(solution)/shard_map/ppermute | solution.py:12
  214.5 3.5 collective-permute-start.7
  251.8 30.0 %collective-permute-start.10 = (f32[48,48,128]{2,1,0:T(8,128)}, f32[48,48,128]{2,1,0:T(8,128)}, u32[]{:S(2)}, u32[]{:S(2)}) collective-permute-start(f32[48,48,128]{2,1,0:T(8,128)} %copy.33), channel_id=1, source_target_pairs={{0,64},{4,68},{8,72},{12,76},{16,80},{20,84},{24,88},{28,92},{32,9... | collective-permute-start | bytes 3538952 | tf_op jit(solution)/shard_map/ppermute | solution.py:12
  261.0 20.6 collective-permute-start.9
  297.6 338.9 %collective-permute-start.11 = (f32[48,48,128]{2,1,0:T(8,128)}, f32[48,48,128]{2,1,0:T(8,128)}, u32[]{:S(2)}, u32[]{:S(2)}) collective-permute-start(f32[48,48,128]{2,1,0:T(8,128)} %copy.36), channel_id=1, source_target_pairs={{0,128},{4,132},{8,136},{12,140},{16,144},{20,148},{24,152},{28,15... | collective-permute-start | bytes 3538952 | tf_op jit(solution)/shard_map/ppermute | solution.py:12
  313.1 350.7 %collective-permute-start.15 = (f32[48,48,128]{2,1,0:T(8,128)}, f32[48,48,128]{2,1,0:T(8,128)}, u32[]{:S(2)}, u32[]{:S(2)}) collective-permute-start(f32[48,48,128]{2,1,0:T(8,128)} %copy.40), channel_id=1, source_target_pairs={{4,0},{8,4},{12,8},{16,12},{20,16},{24,20},{28,24},{32,28},{36,32}... | collective-permute-start | bytes 3538952 | tf_op jit(solution)/shard_map/ppermute | solution.py:12
  649.2 3.8 collective-permute-start.12
  655.3 4.9 collective-permute-start.13
  662.5 5.5 collective-permute-start.14
  680.0 30.3 %collective-permute-start.17 = (f32[48,48,128]{2,1,0:T(8,128)}, f32[48,48,128]{2,1,0:T(8,128)}, u32[]{:S(2)}, u32[]{:S(2)}) collective-permute-start(f32[48,48,128]{2,1,0:T(8,128)} %copy.42), channel_id=1, source_target_pairs={{8,0},{12,4},{16,8},{20,12},{24,16},{28,20},{32,24},{36,28},{40,32... | collective-permute-start | bytes 3538952 | tf_op jit(solution)/shard_map/ppermute | solution.py:12
  681.3 9.2 collective-permute-start.16
  726.1 21.3 collective-permute-start.19
  727.4 7.2 collective-permute-start.18
  763.3 18.8 collective-permute-start.21
  764.7 13.6 collective-permute-start.20
  798.0 17.5 collective-permute-start.23
  799.4 6.5 collective-permute-start.22
  831.5 344.5 %collective-permute-start.24 = (f32[48,48,128]{2,1,0:T(8,128)}, f32[48,48,128]{2,1,0:T(8,128)}, u32[]{:S(2)}, u32[]{:S(2)}) collective-permute-start(f32[48,48,128]{2,1,0:T(8,128)} %copy.54), channel_id=1, source_target_pairs={{128,0},{132,4},{136,8},{140,12},{144,16},{148,20},{152,24},{156,2... | collective-permute-start | bytes 3538952 | tf_op jit(solution)/shard_map/ppermute | solution.py:12
  1179.3 128.4 %copy-start.9 = (f32[1,48,1,128]{3,2,1,0:T(1,128)S(1)}, f32[1,48,1,128]{3,2,1,0:T(1,128)}, u32[]{:S(2)}) copy-start(f32[1,48,1,128]{3,2,1,0:T(1,128)} %param.6) | copy-start | bytes 73732
  1188.6 4.9 collective-permute-start.25
  1195.8 110.7 %collective-permute-start.27 = (f32[1,48,1,128]{3,1,2,0:T(8,128)S(1)}, f32[1,48,1,128]{3,1,2,0:T(8,128)S(1)}, u32[]{:S(2)}, u32[]{:S(2)}) collective-permute-start(f32[1,48,1,128]{3,1,2,0:T(8,128)S(1)} %subtract_bitcast_fusion.5), channel_id=1, source_target_pairs={{1,0},{2,1},{3,2},{5,4},{6,5},{7,6},{9,8},{10,9},{11,10},{13,12},{... | collective-permute-start | bytes 73736 | tf_op jit(solution)/shard_map/ppermute | solution.py:28
  1304.6 3.1 collective-permute-start.26
  1308.9 2.3 collective-permute-start.28
  1313.5 4.3 collective-permute-start.29
  1318.9 15.3 copy-start
  1319.0 6.7 collective-permute-start.30
  1328.2 5.8 collective-permute-start.31
  1335.2 12.3 copy-start.1
  1335.2 4.6 collective-permute-start.32
  1342.4 4.9 collective-permute-start.33
  1648.6 19.9 copy-start.2
  1651.2 2.2 collective-permute-start.34
  1655.8 4.8 collective-permute-start.35
  1663.0 5.5 collective-permute-start.36
  1669.5 18.2 copy-start.3
  1669.6 9.0 collective-permute-start.37
  1681.3 6.4 collective-permute-start.38
  1688.7 13.8 copy-start.4
  1688.8 5.0 collective-permute-start.39
  1696.4 6.1 collective-permute-start.40
  1703.6 303.9 %copy-start.7 = (bf16[128,48,48]{2,1,0:T(8,128)(2,1)S(1)}, bf16[128,48,48]{2,1,0:T(8,128)(2,1)}, u32[]{:S(2)}) copy-start(bf16[128,48,48]{2,1,0:T(8,128)(2,1)} %copy.127) | copy-start | bytes 1769476
  2002.8 4.6 collective-permute-start.41
  2008.5 131.9 %collective-permute-start.43 = (f32[1,48,1,128]{3,1,2,0:T(8,128)S(1)}, f32[1,48,1,128]{3,1,2,0:T(8,128)S(1)}, u32[]{:S(2)}, u32[]{:S(2)}) collective-permute-start(f32[1,48,1,128]{3,1,2,0:T(8,128)S(1)} %subtract_bitcast_fusion.4), channel_id=1, source_target_pairs={{1,0},{2,1},{3,2},{5,4},{6,5},{7,6},{9,8},{10,9},{11,10},{13,12},{... | collective-permute-start | bytes 73736 | tf_op jit(solution)/shard_map/ppermute | solution.py:28
  2137.3 4.1 collective-permute-start.42
where the time goes:
time: 2150 us; the launch traced here: 2140 us
  blocking collectives  1260 us (59%)
  starting transfers between devices  397 us (18%)
  waiting for transfers between devices  240 us (11%)
  matrix products  106 us (5%)
  local copies, waits for them, and re-layouts  90.9 us (4%)
  other arithmetic  47 us (2%)
    psum x4, blocking collectives, from_root(): return lax.psum(jnp.where(mine, shard, jnp.zeros_like(shard)), axis)  1260 us
    ppermute x40, waiting for transfers between devices, from_behind(): lax.ppermute(value, axis, [(source, source + steps) for source in range(i...  238 us
    ppermute x2, starting transfers between devices, extended(): lax.ppermute(lax.slice_in_dim(block, 0, width, axis=dim), axis, backward)  237 us
    ppermute x40, starting transfers between devices, from_behind(): lax.ppermute(value, axis, [(source, source + steps) for source in range(i...  155 us
    dot_general x12, matrix products, doubling_maps(): jnp.einsum('bcl,cal->bal', current, moved, precision=highest)  106 us
  transfers between devices with their start and end apart: 44, of which 35 were waited for; matrix products, arithmetic and copies ran while one was open for 2% of the time, Pallas kernels for 0%

commit v1 on v0

--- a/solution.py
+++ b/solution.py
@@ -4,6 +4,12 @@
 from jax.sharding import PartitionSpec as P
 
 highest = lax.Precision.HIGHEST
+
+
+def add_all(x, axis):
+    shards = lax.all_gather(x, axis, axis=0, tiled=False)
+    summed = shards.sum(axis=0)
+    return summed
 
 
 def from_behind(value, axis, steps):
@@ -14,7 +20,7 @@
 
 def from_root(shard, axis, root):
     mine = lax.axis_index(axis) == root
-    return lax.psum(jnp.where(mine, shard, jnp.zeros_like(shard)), axis)
+    return add_all(jnp.where(mine, shard, jnp.zeros_like(shard)), axis)
 
 
 def extended(block, sides, width):

time: 2150 us -> 1260 us (0.59)
  blocking collectives: 1260 us -> 0 us
  waiting for transfers between devices: 240 us -> 788 us
  starting transfers between devices: 397 us -> 198 us
    psum x4 -> x0, blocking collectives: 1260 us -> none  [from_root(): return lax.psum(jnp.where(mine, shard, jnp.zeros_like(shard)), axis)]
    all_gather x0 -> x4, waiting for transfers between devices: none -> 492 us  [add_all(): shards = lax.all_gather(x, axis, axis=0, tiled=False)]
    ppermute x2, starting transfers between devices: 237 us -> 14.5 us  [extended(): lax.ppermute(lax.slice_in_dim(block, 0, width, axis=dim), axis, backward)]
    ppermute x40, waiting for transfers between devices: 238 us -> 294 us  [from_behind(): lax.ppermute(value, axis, [(source, source + steps) for source in range(i...]
    ppermute x40, starting transfers between devices: 155 us -> 179 us  [from_behind(): lax.ppermute(value, axis, [(source, source + steps) for source in range(i...]
  transfers between devices with their start and end apart: 44 -> 48, of which waited for: 35 -> 40; matrix products, arithmetic and copies ran while one was open for 2% -> 4% of each run, Pallas kernels for 0% -> 0%
where the time goes in v1:
time: 1260 us; the launch traced here: 1250 us
  waiting for transfers between devices  788 us (63%)
  starting transfers between devices  198 us (16%)
  matrix products  106 us (8%)
  local copies, waits for them, and re-layouts  90.8 us (7%)
  other arithmetic  55.6 us (4%)
  between operations  15.1 us (1%)
    all_gather x4, waiting for transfers between devices, add_all(): shards = lax.all_gather(x, axis, axis=0, tiled=False)  492 us
    ppermute x40, waiting for transfers between devices, from_behind(): lax.ppermute(value, axis, [(source, source + steps) for source in range(i...  294 us
    ppermute x40, starting transfers between devices, from_behind(): lax.ppermute(value, axis, [(source, source + steps) for source in range(i...  179 us
    dot_general x12, matrix products, doubling_maps(): jnp.einsum('bcl,cal->bal', current, moved, precision=highest)  106 us
    ppermute x12, local copies, waits for them, and re-layouts, from_behind(): lax.ppermute(value, axis, [(source, source + steps) for source in range(i...  39.4 us
    unnamed x26, other arithmetic  38 us
    select_n x10, local copies, waits for them, and re-layouts, doubling_maps(): jnp.where(exists, jnp.einsum('bcl,cal->bal', current, moved, precision=hi...  31 us
  transfers between devices with their start and end apart: 48, of which 40 were waited for; matrix products, arithmetic and copies ran while one was open for 4% of the time, Pallas kernels for 0%

profile of v1, /device:TPU:1, one launch (start us, length us, event | category | flops | bytes accessed | tf_op | source)
XLA Modules:
  0.0 1253.4 jit_solution(11771890342905836268)
XLA Ops:
  14.3 5.4 collective-permute-start.2
  26.1 17.9 %collective-permute-done = f32[48,128]{1,0:T(8,128)S(1)} collective-permute-done((f32[48,128]{1,0:T(8,128)S(1)}, f32[48,128]{1,0:T(8,128)S(1)}, u32[]{:S(2)}, u32[]{:S(2)}) %collective-permute-start) | collective-permute-done | bytes 24608 | tf_op jit(solution)/shard_map/ppermute | solution.py:18
  45.2 5.6 collective-permute-start.1
  55.1 7.0 multiply_reduce_fusion.26
  64.1 8.3 collective-permute-start.4
  72.5 5.2 collective-permute-start.3
  77.7 42.6 %collective-permute-done.3 = f32[48,128]{1,0:T(8,128)S(1)} collective-permute-done((f32[48,128]{1,0:T(8,128)S(1)}, f32[48,128]{1,0:T(8,128)S(1)}, u32[]{:S(2)}, u32[]{:S(2)}) %collective-permute-start.3) | collective-permute-done | bytes 24608 | tf_op jit(solution)/shard_map/ppermute | solution.py:18
  123.7 6.5 multiply_reduce_fusion.25
  133.4 9.1 collective-permute-start.6
  142.6 6.0 collective-permute-start.5
  149.6 17.3 %collective-permute-done.6 = f32[48,48,128]{2,1,0:T(8,128)} collective-permute-done((f32[48,48,128]{2,1,0:T(8,128)}, f32[48,48,128]{2,1,0:T(8,128)}, u32[]{:S(2)}, u32[]{:S(2)}) %collective-permute-start.6) | collective-permute-done | bytes 1179680 | tf_op jit(solution)/shard_map/ppermute | solution.py:18
  166.9 3.3 copy.28
  170.2 9.3 multiply_reduce_fusion.24
  182.8 38.2 %collective-permute-start.8 = (f32[48,48,128]{2,1,0:T(8,128)}, f32[48,48,128]{2,1,0:T(8,128)}, u32[]{:S(2)}, u32[]{:S(2)}) collective-permute-start(f32[48,48,128]{2,1,0:T(8,128)} %copy.30), channel_id=1, source_target_pairs={{0,32},{4,36},{8,40},{12,44},{16,48},{20,52},{24,56},{28,60},{32,6... | collective-permute-start | bytes 3538952 | tf_op jit(solution)/shard_map/ppermute | solution.py:18
  224.7 17.8 %collective-permute-done.8 = f32[48,48,128]{2,1,0:T(8,128)} collective-permute-done((f32[48,48,128]{2,1,0:T(8,128)}, f32[48,48,128]{2,1,0:T(8,128)}, u32[]{:S(2)}, u32[]{:S(2)}) %collective-permute-start.8) | collective-permute-done | bytes 1179680 | tf_op jit(solution)/shard_map/ppermute | solution.py:18
  245.7 9.4 multiply_reduce_fusion.23
  258.4 9.1 collective-permute-start.10
  267.6 3.7 collective-permute-start.9
  271.2 17.0 %collective-permute-done.9 = f32[48,128]{1,0:T(8,128)S(1)} collective-permute-done((f32[48,128]{1,0:T(8,128)S(1)}, f32[48,128]{1,0:T(8,128)S(1)}, u32[]{:S(2)}, u32[]{:S(2)}) %collective-permute-start.9) | collective-permute-done | bytes 24608 | tf_op jit(solution)/shard_map/ppermute | solution.py:18
  288.3 3.3 copy.34
  291.6 9.3 multiply_reduce_fusion.22
  304.9 6.4 collective-permute-start.11
  313.9 3.3 fusion.9
  324.7 5.7 collective-permute-done.11
  330.4 3.3 copy.37
  333.7 90.8 %all-gather.9.cloned.1.call-done = f32[3072,128]{1,0:T(8,128)} async-done(((f32[48,128]{1,0:T(8,128)}), f32[3072,128]{1,0:T(8,128)}) %all-gather.9.cloned.1.call-update) | async-done | bytes 1572880 | tf_op jit(solution)/shard_map/all_gather | solution.py:10
  426.2 9.3 multiply_reduce_fusion.21
  443.7 3.3 collective-permute-done.13
  450.8 3.3 copy.41
  454.9 8.6 multiply_reduce_fusion.19
  463.5 3.3 copy.42
  469.5 9.3 collective-permute-done.16
  478.9 40.2 %collective-permute-done.17 = f32[48,48,128]{2,1,0:T(8,128)} collective-permute-done((f32[48,48,128]{2,1,0:T(8,128)}, f32[48,48,128]{2,1,0:T(8,128)}, u32[]{:S(2)}, u32[]{:S(2)}) %collective-permute-start.17) | collective-permute-done | bytes 1179680 | tf_op jit(solution)/shard_map/ppermute | solution.py:18
  522.3 9.3 multiply_reduce_fusion.18
  537.7 10.4 collective-permute-done.18
  548.2 14.5 %collective-permute-done.19 = f32[48,48,128]{2,1,0:T(8,128)} collective-permute-done((f32[48,48,128]{2,1,0:T(8,128)}, f32[48,48,128]{2,1,0:T(8,128)}, u32[]{:S(2)}, u32[]{:S(2)}) %collective-permute-start.19) | collective-permute-done | bytes 1179680 | tf_op jit(solution)/shard_map/ppermute | solution.py:18
  562.7 3.3 copy.46
  566.1 9.5 multiply_reduce_fusion.17
  581.5 17.0 %collective-permute-done.20 = f32[48,128]{1,0:T(8,128)S(1)} collective-permute-done((f32[48,128]{1,0:T(8,128)S(1)}, f32[48,128]{1,0:T(8,128)S(1)}, u32[]{:S(2)}, u32[]{:S(2)}) %collective-permute-start.20) | collective-permute-done | bytes 24608 | tf_op jit(solution)/shard_map/ppermute | solution.py:18
  598.6 3.3 copy.49
  601.9 9.4 multiply_reduce_fusion.16
  617.6 4.4 collective-permute-done.22
  622.0 9.7 collective-permute-done.23
  635.0 9.5 multiply_reduce_fusion.15
  649.8 17.5 %collective-permute-done.24 = f32[48,48,128]{2,1,0:T(8,128)} collective-permute-done((f32[48,48,128]{2,1,0:T(8,128)}, f32[48,48,128]{2,1,0:T(8,128)}, u32[]{:S(2)}, u32[]{:S(2)}) %collective-permute-start.24) | collective-permute-done | bytes 1179680 | tf_op jit(solution)/shard_map/ppermute | solution.py:18
  670.5 158.0 %all-gather.11.cloned.1.call-done = f32[3072,128]{1,0:T(8,128)} async-done(((f32[48,128]{1,0:T(8,128)}), f32[3072,128]{1,0:T(8,128)}) %all-gather.11.cloned.1.call-update) | async-done | bytes 1572880 | tf_op jit(solution)/shard_map/all_gather | solution.py:10
  830.2 9.3 multiply_reduce_fusion.14
  840.8 3.3 collective-permute-done.25
  846.4 7.3 collective-permute-start.27
  863.8 5.6 collective-permute-start.29
  871.3 8.6 collective-permute-start.30
  883.4 13.8 %collective-permute-start.31 = (f32[48,128]{1,0:T(8,128)S(1)}, f32[48,128]{1,0:T(8,128)S(1)}, u32[]{:S(2)}, u32[]{:S(2)}) collective-permute-start(f32[48,128]{1,0:T(8,128)S(1)} %bitcast_add_fusion.13), channel_id=1, source_target_pairs={{0,32},{4,36},{8,40},{12,44},{16,48},{20,52},{24,56},{28,60},{32,6... | collective-permute-start | bytes 73736 | tf_op jit(solution)/shard_map/ppermute | solution.py:18
  899.4 8.9 collective-permute-start.32
  911.9 5.1 collective-permute-start.33
  919.8 113.9 %all-gather.13.cloned.1.call-done = f32[3072,128]{1,0:T(8,128)} async-done(((f32[48,128]{1,0:T(8,128)}), f32[3072,128]{1,0:T(8,128)}) %all-gather.13.cloned.1.call-update) | async-done | bytes 1572880 | tf_op jit(solution)/shard_map/all_gather | solution.py:10
  1044.9 3.5 collective-permute-done.35
  1052.1 4.3 collective-permute-done.36
  1059.2 7.2 collective-permute-done.37
  1070.2 6.9 collective-permute-done.38
  1079.9 6.4 collective-permute-done.39
  1090.1 4.8 collective-permute-done.40
  1096.7 129.0 %all-gather.15.cloned.1.call-done = f32[3072,128]{1,0:T(8,128)} async-done(((f32[48,128]{1,0:T(8,128)}), f32[3072,128]{1,0:T(8,128)}) %all-gather.15.cloned.1.call-update) | async-done | bytes 1572880 | tf_op jit(solution)/shard_map/all_gather | solution.py:10
  1231.2 3.3 collective-permute-done.41
  1235.6 7.3 collective-permute-start.43
  (232 shorter events, 175.9 us)
Async XLA Ops:
  7.2 417.4 %all-gather.9.cloned.1.call-start = ((), (), s32[]{:S(2)}) async-start(), calls=%async_computation | async-start | bytes 1597440 | tf_op jit(solution)/shard_map/all_gather | solution.py:10
  9.1 35.1 %copy-start.5 = (bf16[1,48,48,1,128]{2,1,4,3,0:T(8,128)(2,1)}, bf16[1,48,48,1,128]{2,1,4,3,0:T(8,128)(2,1)S(1)}, u32[]{:S(2)}) copy-start(bf16[1,48,48,1,128]{2,1,4,3,0:T(8,128)(2,1)S(1)} %copy.21) | copy-start | bytes 1769476
  11.1 11.2 copy-start.8
  14.3 37.5 %collective-permute-start.2 = (f32[48,48,128]{2,1,0:T(8,128)}, f32[48,48,128]{2,1,0:T(8,128)}, u32[]{:S(2)}, u32[]{:S(2)}) collective-permute-start(f32[48,48,128]{2,1,0:T(8,128)} %copy.22), channel_id=1, source_target_pairs={{0,4},{4,8},{8,12},{12,16},{16,20},{20,24},{24,28},{28,32},{32,36}... | collective-permute-start | bytes 3538952 | tf_op jit(solution)/shard_map/ppermute | solution.py:18
  21.5 30.3 %copy-start.6 = (bf16[128,48,48]{2,1,0:T(8,128)(2,1)}, bf16[128,48,48]{2,1,0:T(8,128)(2,1)S(1)}, u32[]{:S(2)}) copy-start(bf16[128,48,48]{2,1,0:T(8,128)(2,1)S(1)} %copy.68) | copy-start | bytes 1769476
  23.5 20.5 %collective-permute-start = (f32[48,128]{1,0:T(8,128)S(1)}, f32[48,128]{1,0:T(8,128)S(1)}, u32[]{:S(2)}, u32[]{:S(2)}) collective-permute-start(f32[48,128]{1,0:T(8,128)S(1)} %subtract_bitcast_fusion.3), channel_id=1, source_target_pairs={{0,4},{4,8},{8,12},{12,16},{16,20},{20,24},{24,28},{28,32},{32,36}... | collective-permute-start | bytes 73736 | tf_op jit(solution)/shard_map/ppermute | solution.py:18
  45.2 6.5 collective-permute-start.1
  64.1 56.3 %collective-permute-start.4 = (f32[48,48,128]{2,1,0:T(8,128)}, f32[48,48,128]{2,1,0:T(8,128)}, u32[]{:S(2)}, u32[]{:S(2)}) collective-permute-start(f32[48,48,128]{2,1,0:T(8,128)} %copy.24), channel_id=1, source_target_pairs={{0,8},{4,12},{8,16},{12,20},{16,24},{20,28},{24,32},{28,36},{32,40... | collective-permute-start | bytes 3538952 | tf_op jit(solution)/shard_map/ppermute | solution.py:18
  72.5 47.8 %collective-permute-start.3 = (f32[48,128]{1,0:T(8,128)S(1)}, f32[48,128]{1,0:T(8,128)S(1)}, u32[]{:S(2)}, u32[]{:S(2)}) collective-permute-start(f32[48,128]{1,0:T(8,128)S(1)} %bitcast_add_fusion.29), channel_id=1, source_target_pairs={{0,16},{4,20},{8,24},{12,28},{16,32},{20,36},{24,40},{28,44},{32,4... | collective-permute-start | bytes 73736 | tf_op jit(solution)/shard_map/ppermute | solution.py:18
  133.4 33.5 %collective-permute-start.6 = (f32[48,48,128]{2,1,0:T(8,128)}, f32[48,48,128]{2,1,0:T(8,128)}, u32[]{:S(2)}, u32[]{:S(2)}) collective-permute-start(f32[48,48,128]{2,1,0:T(8,128)} %copy.27), channel_id=1, source_target_pairs={{0,16},{4,20},{8,24},{12,28},{16,32},{20,36},{24,40},{28,44},{32,4... | collective-permute-start | bytes 3538952 | tf_op jit(solution)/shard_map/ppermute | solution.py:18
  142.6 6.9 collective-permute-start.5
  182.8 59.7 %collective-permute-start.8 = (f32[48,48,128]{2,1,0:T(8,128)}, f32[48,48,128]{2,1,0:T(8,128)}, u32[]{:S(2)}, u32[]{:S(2)}) collective-permute-start(f32[48,48,128]{2,1,0:T(8,128)} %copy.30), channel_id=1, source_target_pairs={{0,32},{4,36},{8,40},{12,44},{16,48},{20,52},{24,56},{28,60},{32,6... | collective-permute-start | bytes 3538952 | tf_op jit(solution)/shard_map/ppermute | solution.py:18
  221.1 3.5 collective-permute-start.7
  258.4 29.9 %collective-permute-start.10 = (f32[48,48,128]{2,1,0:T(8,128)}, f32[48,48,128]{2,1,0:T(8,128)}, u32[]{:S(2)}, u32[]{:S(2)}) collective-permute-start(f32[48,48,128]{2,1,0:T(8,128)} %copy.33), channel_id=1, source_target_pairs={{0,64},{4,68},{8,72},{12,76},{16,80},{20,84},{24,88},{28,92},{32,9... | collective-permute-start | bytes 3538952 | tf_op jit(solution)/shard_map/ppermute | solution.py:18
  267.6 20.6 %collective-permute-start.9 = (f32[48,128]{1,0:T(8,128)S(1)}, f32[48,128]{1,0:T(8,128)S(1)}, u32[]{:S(2)}, u32[]{:S(2)}) collective-permute-start(f32[48,128]{1,0:T(8,128)S(1)} %bitcast_add_fusion.26), channel_id=1, source_target_pairs={{0,128},{4,132},{8,136},{12,140},{16,144},{20,148},{24,152},{28,15... | collective-permute-start | bytes 73736 | tf_op jit(solution)/shard_map/ppermute | solution.py:18
  301.6 526.9 %all-gather.11.cloned.1.call-start = ((), (), s32[]{:S(2)}) async-start(), calls=%async_computation.1 | async-start | bytes 1597440 | tf_op jit(solution)/shard_map/all_gather | solution.py:10
  304.9 25.5 %collective-permute-start.11 = (f32[48,48,128]{2,1,0:T(8,128)}, f32[48,48,128]{2,1,0:T(8,128)}, u32[]{:S(2)}, u32[]{:S(2)}) collective-permute-start(f32[48,48,128]{2,1,0:T(8,128)} %copy.36), channel_id=1, source_target_pairs={{0,128},{4,132},{8,136},{12,140},{16,144},{20,148},{24,152},{28,15... | collective-permute-start | bytes 3538952 | tf_op jit(solution)/shard_map/ppermute | solution.py:18
  320.4 130.4 %collective-permute-start.15 = (f32[48,48,128]{2,1,0:T(8,128)}, f32[48,48,128]{2,1,0:T(8,128)}, u32[]{:S(2)}, u32[]{:S(2)}) collective-permute-start(f32[48,48,128]{2,1,0:T(8,128)} %copy.40), channel_id=1, source_target_pairs={{4,0},{8,4},{12,8},{16,12},{20,16},{24,20},{28,24},{32,28},{36,32}... | collective-permute-start | bytes 3538952 | tf_op jit(solution)/shard_map/ppermute | solution.py:18
  435.6 4.5 collective-permute-start.12
  442.4 4.6 collective-permute-start.13
  449.3 5.5 collective-permute-start.14
  466.8 52.2 %collective-permute-start.17 = (f32[48,48,128]{2,1,0:T(8,128)}, f32[48,48,128]{2,1,0:T(8,128)}, u32[]{:S(2)}, u32[]{:S(2)}) collective-permute-start(f32[48,48,128]{2,1,0:T(8,128)} %copy.42), channel_id=1, source_target_pairs={{8,0},{12,4},{16,8},{20,12},{24,16},{28,20},{32,24},{36,28},{40,32... | collective-permute-start | bytes 3538952 | tf_op jit(solution)/shard_map/ppermute | solution.py:18
  468.2 10.6 collective-permute-start.16
  534.8 27.9 %collective-permute-start.19 = (f32[48,48,128]{2,1,0:T(8,128)}, f32[48,48,128]{2,1,0:T(8,128)}, u32[]{:S(2)}, u32[]{:S(2)}) collective-permute-start(f32[48,48,128]{2,1,0:T(8,128)} %copy.45), channel_id=1, source_target_pairs={{16,0},{20,4},{24,8},{28,12},{32,16},{36,20},{40,24},{44,28},{48,3... | collective-permute-start | bytes 3538952 | tf_op jit(solution)/shard_map/ppermute | solution.py:18
  536.2 12.0 collective-permute-start.18
  578.8 19.8 %collective-permute-start.21 = (f32[48,48,128]{2,1,0:T(8,128)}, f32[48,48,128]{2,1,0:T(8,128)}, u32[]{:S(2)}, u32[]{:S(2)}) collective-permute-start(f32[48,48,128]{2,1,0:T(8,128)} %copy.48), channel_id=1, source_target_pairs={{32,0},{36,4},{40,8},{44,12},{48,16},{52,20},{56,24},{60,28},{64,3... | collective-permute-start | bytes 3538952 | tf_op jit(solution)/shard_map/ppermute | solution.py:18
  580.2 18.3 %collective-permute-start.20 = (f32[48,128]{1,0:T(8,128)S(1)}, f32[48,128]{1,0:T(8,128)S(1)}, u32[]{:S(2)}, u32[]{:S(2)}) collective-permute-start(f32[48,128]{1,0:T(8,128)S(1)} %bitcast_add_fusion.20), channel_id=1, source_target_pairs={{64,0},{68,4},{72,8},{76,12},{80,16},{84,20},{88,24},{92,28},{96,3... | collective-permute-start | bytes 73736 | tf_op jit(solution)/shard_map/ppermute | solution.py:18
  614.5 17.3 %collective-permute-start.23 = (f32[48,48,128]{2,1,0:T(8,128)}, f32[48,48,128]{2,1,0:T(8,128)}, u32[]{:S(2)}, u32[]{:S(2)}) collective-permute-start(f32[48,48,128]{2,1,0:T(8,128)} %copy.51), channel_id=1, source_target_pairs={{64,0},{68,4},{72,8},{76,12},{80,16},{84,20},{88,24},{92,28},{96,3... | collective-permute-start | bytes 3538952 | tf_op jit(solution)/shard_map/ppermute | solution.py:18
  615.9 6.1 collective-permute-start.22
  645.2 388.5 %all-gather.13.cloned.1.call-start = ((), (), s32[]{:S(2)}) async-start(), calls=%async_computation.2 | async-start | bytes 1597440 | tf_op jit(solution)/shard_map/all_gather | solution.py:10
  648.5 18.8 %collective-permute-start.24 = (f32[48,48,128]{2,1,0:T(8,128)}, f32[48,48,128]{2,1,0:T(8,128)}, u32[]{:S(2)}, u32[]{:S(2)}) collective-permute-start(f32[48,48,128]{2,1,0:T(8,128)} %copy.54), channel_id=1, source_target_pairs={{128,0},{132,4},{136,8},{140,12},{144,16},{148,20},{152,24},{156,2... | collective-permute-start | bytes 3538952 | tf_op jit(solution)/shard_map/ppermute | solution.py:18
  830.2 26.6 %copy-start.9 = (f32[1,48,1,128]{3,2,1,0:T(1,128)S(1)}, f32[1,48,1,128]{3,2,1,0:T(1,128)}, u32[]{:S(2)}) copy-start(f32[1,48,1,128]{3,2,1,0:T(1,128)} %param.6) | copy-start | bytes 73732
  839.5 4.6 collective-permute-start.25
  846.4 9.4 collective-permute-start.27
  853.7 3.1 collective-permute-start.26
  858.0 3.4 collective-permute-start.28
  863.8 6.3 collective-permute-start.29
  871.2 27.1 %copy-start = (f32[48,48,128]{0,1,2:T(8,128)S(1)}, f32[48,48,128]{0,1,2:T(8,128)}, u32[]{:S(2)}) copy-start(f32[48,48,128]{0,1,2:T(8,128)} %get-tuple-element.13) | copy-start | bytes 3538948
  871.3 9.6 collective-permute-start.30
  883.4 14.8 %collective-permute-start.31 = (f32[48,128]{1,0:T(8,128)S(1)}, f32[48,128]{1,0:T(8,128)S(1)}, u32[]{:S(2)}, u32[]{:S(2)}) collective-permute-start(f32[48,128]{1,0:T(8,128)S(1)} %bitcast_add_fusion.13), channel_id=1, source_target_pairs={{0,32},{4,36},{8,40},{12,44},{16,48},{20,52},{24,56},{28,60},{32,6... | collective-permute-start | bytes 73736 | tf_op jit(solution)/shard_map/ppermute | solution.py:18
  899.3 18.7 %copy-start.1 = (f32[48,48,128]{0,1,2:T(8,128)S(1)}, f32[48,48,128]{0,1,2:T(8,128)}, u32[]{:S(2)}) copy-start(f32[48,48,128]{0,1,2:T(8,128)} %get-tuple-element.17) | copy-start | bytes 3538948
  899.4 9.8 collective-permute-start.32
  911.9 6.1 collective-permute-start.33
  919.7 306.0 %all-gather.15.cloned.1.call-start = ((), (), s32[]{:S(2)}) async-start(), calls=%async_computation.3 | async-start | bytes 1597440 | tf_op jit(solution)/shard_map/all_gather | solution.py:10
  1035.3 21.1 %copy-start.2 = (f32[48,48,128]{0,1,2:T(8,128)S(1)}, f32[48,48,128]{0,1,2:T(8,128)}, u32[]{:S(2)}) copy-start(f32[48,48,128]{0,1,2:T(8,128)} %get-tuple-element.21) | copy-start | bytes 3538948
  1038.0 3.3 collective-permute-start.34
  1043.6 4.8 collective-permute-start.35
  1050.8 5.6 collective-permute-start.36
  1057.5 19.7 %copy-start.3 = (f32[48,48,128]{0,1,2:T(8,128)S(1)}, f32[48,48,128]{0,1,2:T(8,128)}, u32[]{:S(2)}) copy-start(f32[48,48,128]{0,1,2:T(8,128)} %get-tuple-element.25) | copy-start | bytes 3538948
  1057.6 8.7 collective-permute-start.37
  1068.9 8.2 collective-permute-start.38
  1078.2 16.8 %copy-start.4 = (f32[48,48,128]{0,1,2:T(8,128)S(1)}, f32[48,48,128]{0,1,2:T(8,128)}, u32[]{:S(2)}) copy-start(f32[48,48,128]{0,1,2:T(8,128)} %get-tuple-element.29) | copy-start | bytes 3538948
  1078.3 7.9 collective-permute-start.39
  1088.8 6.1 collective-permute-start.40
  1096.0 138.5 %copy-start.7 = (bf16[128,48,48]{2,1,0:T(8,128)(2,1)S(1)}, bf16[128,48,48]{2,1,0:T(8,128)(2,1)}, u32[]{:S(2)}) copy-start(bf16[128,48,48]{2,1,0:T(8,128)(2,1)} %copy.127) | copy-start | bytes 1769476
  1229.9 4.6 collective-permute-start.41
  1235.6 9.4 collective-permute-start.43
  1242.9 3.1 collective-permute-start.42
Sparse Core Ops, SparseCore 0:
  301.7 122.7 all-gather.8
  645.3 183.1 all-gather.10
  919.9 113.8 all-gather.12
  1096.9 128.8 all-gather.14
